TPU v7x, 32 devices: a whole 2x2x4 slice. The times are simulated.
32 devices in a mesh: dp: 4 (over y, x), tensor: 8 (over z, core).
Axes of the slice: x: 2, y: 2, z: 4, core: 2. Of those that a mesh axis runs over, the one named last changes fastest.
Arguments:
- inputs: bfloat16 [16384, 2048], P(('dp', 'tensor')), may hold values from -6 to 6
- block_ids: int32 [16, 1024], P('dp'), may hold values from 0 to 4, never falling along the last dimension, each value on 1 to 256 neighbouring positions
- norm_gain: bfloat16 [2048], replicated, may hold values from 0.5 to 1.5
- norm_bias: bfloat16 [2048], replicated, may hold values from -3 to 3
- query_weight: bfloat16 [2048, 2048], P('dp', 'tensor'), may hold values from -0.125 to 0.125
- query_bias: bfloat16 [2048], P('tensor'), may hold values from -3 to 3
- key_weight: bfloat16 [2048, 2048], P('dp', 'tensor'), may hold values from -0.125 to 0.125
- key_bias: bfloat16 [2048], P('tensor'), may hold values from -3 to 3
- value_weight: bfloat16 [2048, 2048], P('dp', 'tensor'), may hold values from -0.125 to 0.125
- value_bias: bfloat16 [2048], P('tensor'), may hold values from -3 to 3
- out_weight: bfloat16 [2048, 2048], P('tensor', 'dp'), may hold values from -3 to 3
- out_bias: bfloat16 [2048], replicated, may hold values from -3 to 3
- up_weight: bfloat16 [2048, 8192], P('dp', 'tensor'), may hold values from -0.125 to 0.125
- up_bias: bfloat16 [8192], P('tensor'), may hold values from -3 to 3
- down_weight: bfloat16 [8192, 2048], P('tensor', 'dp'), may hold values from -0.09375 to 0.09375
- down_bias: bfloat16 [2048], replicated, may hold values from -3 to 3
- grad_out: bfloat16 [16384, 2048], P(('dp', 'tensor')), may hold values from -6 to 6
Outputs:
- output: bfloat16 [16384, 2048], P(('dp', 'tensor'))
- input_grad: bfloat16 [16384, 2048], P(('dp', 'tensor'))
- norm_gain_grad: float32 [2048], replicated
- norm_bias_grad: float32 [2048], replicated
- query_weight_grad: float32 [2048, 2048], P('dp', 'tensor')
- query_bias_grad: float32 [2048], P('tensor')
- key_weight_grad: float32 [2048, 2048], P('dp', 'tensor')
- key_bias_grad: float32 [2048], P('tensor')
- value_weight_grad: float32 [2048, 2048], P('dp', 'tensor')
- value_bias_grad: float32 [2048], P('tensor')
- out_weight_grad: float32 [2048, 2048], P('tensor', 'dp')
- out_bias_grad: float32 [2048], replicated
- up_weight_grad: float32 [2048, 8192], P('dp', 'tensor')
- up_bias_grad: float32 [8192], P('tensor')
- down_weight_grad: float32 [8192, 2048], P('tensor', 'dp')
- down_bias_grad: float32 [2048], replicated
Inputs may be any that keep to these rules, and one draw needn't show every extreme that they name: `block_ids`: in each sequence the block numbers never fall along the positions; a block spans 1 to 256 positions, and one block of each sequence spans exactly 256.
All inputs are finite; a program needn't handle non-finite values.
Results may differ from a plain program's by a relative error of at most 0.012.
The roundings to bfloat16 on the way count: a program that leaves them out, or rounds other values in their place, can miss the bound.
Values may be sent and summed in bfloat16 or wider, within the bound.
A program may use at most 320 MiB of HBM per device.

v0:
```python
import jax
import jax.numpy as jnp
from jax import lax
from jax.sharding import PartitionSpec as P

HEAD_DIM = 64
ROT = 32
eps_norm = 1e-05


def normalize(values, gain_in, shift_in):
    center = jnp.mean(values, axis=-1, keepdims=True)
    centered = values - center
    variance = jnp.mean(centered * centered, axis=-1, keepdims=True)
    return centered * lax.rsqrt(variance + eps_norm) * gain_in + shift_in


def rotary_tables(length, rot_width):
    halves = rot_width // 2
    exponent = jnp.arange(halves, dtype=jnp.float32) * (2.0 / rot_width)
    frequency = jnp.power(10000.0, -exponent)
    angles = jnp.arange(length, dtype=jnp.float32)[:, None] * frequency[None, :]
    angles = jnp.concatenate([angles, angles], axis=1)
    return (jnp.cos(angles), jnp.sin(angles))


def rotate(per_head, cos_table, sin_table):
    rot_width = cos_table.shape[-1]
    halves = rot_width // 2
    first_half = per_head[..., :halves]
    second_half = per_head[..., halves:rot_width]
    turned = jnp.concatenate([-second_half, first_half], axis=-1)
    rotated = per_head[..., :rot_width] * cos_table[:, None, :] + turned * sin_table[:, None, :]
    return jnp.concatenate([rotated, per_head[..., rot_width:]], axis=-1)


def masked_scores(query_block, key_block, query_ids, key_ids):
    raw_scores = jnp.einsum(
        "qhd,khd->hqk", query_block, key_block, preferred_element_type=jnp.float32
    ) * HEAD_DIM ** (-0.5)
    allowed = key_ids[None, None, :] <= query_ids[None, :, None]
    return jnp.where(allowed, raw_scores, -1000000000.0)


def gelu_tanh(values):
    return jax.nn.gelu(values, approximate=True)


def per_device(
    inputs,
    block_ids,
    norm_gain,
    norm_bias,
    query_weight,
    query_bias,
    key_weight,
    key_bias,
    value_weight,
    value_bias,
    out_weight,
    out_bias,
    up_weight,
    up_bias,
    down_weight,
    down_bias,
    grad_out,
):
    seq_count, length = block_ids.shape
    local_width = query_weight.shape[1]
    local_heads = local_width // HEAD_DIM
    block_rows = min(512, length)
    per_sequence = length // block_rows
    all_rows = seq_count * length
    score_scale = HEAD_DIM ** (-0.5)
    gain_float = norm_gain.astype(jnp.float32)
    shift_float = norm_bias.astype(jnp.float32)
    inputs_float = inputs.astype(jnp.float32)
    normed = normalize(inputs_float, gain_float, shift_float).astype(jnp.bfloat16)
    full_query, full_key, full_value, full_up, full_out, full_down = (
        lax.all_gather(query_weight, "dp", axis=0, tiled=True),
        lax.all_gather(key_weight, "dp", axis=0, tiled=True),
        lax.all_gather(value_weight, "dp", axis=0, tiled=True),
        lax.all_gather(up_weight, "dp", axis=0, tiled=True),
        lax.all_gather(out_weight, "dp", axis=1, tiled=True),
        lax.all_gather(down_weight, "dp", axis=1, tiled=True),
    )
    group_rows = lax.all_gather(normed, "tensor", axis=0, tiled=True)
    cos_table, sin_table = rotary_tables(length, ROT)

    def project(weight_part, bias_part):
        return jnp.dot(
            group_rows, weight_part, preferred_element_type=jnp.float32
        ) + bias_part.astype(jnp.float32)

    def split_heads(values):
        return values.reshape(seq_count, length, local_heads, HEAD_DIM)

    queries = rotate(split_heads(project(full_query, query_bias)), cos_table, sin_table).astype(
        jnp.bfloat16
    )
    key_rows = rotate(split_heads(project(full_key, key_bias)), cos_table, sin_table).astype(
        jnp.bfloat16
    )
    value_rows = split_heads(project(full_value, value_bias)).astype(jnp.bfloat16)

    def forward_block(block_index):
        sequence = block_index // per_sequence
        offset = block_index % per_sequence * block_rows
        seq_ids = block_ids[sequence]
        query_block = lax.dynamic_slice_in_dim(queries[sequence], offset, block_rows, 0)
        query_ids = lax.dynamic_slice_in_dim(seq_ids, offset, block_rows, 0)
        scores = masked_scores(query_block, key_rows[sequence], query_ids, seq_ids)
        highest = jnp.max(scores, axis=2, keepdims=True)
        shifted = jnp.exp(scores - highest)
        totals = jnp.sum(shifted, axis=2, keepdims=True)
        weights_low = (shifted / totals).astype(jnp.bfloat16)
        mixed_rows = jnp.einsum(
            "hqk,khd->qhd", weights_low, value_rows[sequence], preferred_element_type=jnp.float32
        )
        return (mixed_rows, (highest + jnp.log(totals))[:, :, 0])

    attended, log_sums = lax.map(forward_block, jnp.arange(seq_count * per_sequence))
    attended_low = attended.reshape(all_rows, local_width).astype(jnp.bfloat16)
    hidden = project(full_up, up_bias)
    active = gelu_tanh(hidden).astype(jnp.bfloat16)
    branch_rows = lax.psum_scatter(
        jnp.dot(attended_low, full_out, preferred_element_type=jnp.float32)
        + jnp.dot(active, full_down, preferred_element_type=jnp.float32),
        "tensor",
        scatter_dimension=0,
        tiled=True,
    )
    output = (
        inputs_float + branch_rows + out_bias.astype(jnp.float32) + down_bias.astype(jnp.float32)
    ).astype(jnp.bfloat16)
    back_query, back_key, back_value, back_up, back_out, back_down = (
        lax.all_gather(query_weight, "dp", axis=0, tiled=True),
        lax.all_gather(key_weight, "dp", axis=0, tiled=True),
        lax.all_gather(value_weight, "dp", axis=0, tiled=True),
        lax.all_gather(up_weight, "dp", axis=0, tiled=True),
        lax.all_gather(out_weight, "dp", axis=1, tiled=True),
        lax.all_gather(down_weight, "dp", axis=1, tiled=True),
    )
    back_rows = lax.all_gather(normed, "tensor", axis=0, tiled=True)
    upstream = lax.all_gather(grad_out, "tensor", axis=0, tiled=True)
    out_wgrad = jnp.einsum("rk,rd->kd", attended_low, upstream, preferred_element_type=jnp.float32)
    down_wgrad = jnp.einsum("rf,rd->fd", active, upstream, preferred_element_type=jnp.float32)
    attended_grad = jnp.einsum(
        "rd,kd->rk", upstream, back_out, preferred_element_type=jnp.float32
    ).astype(jnp.bfloat16)
    active_grad = jnp.einsum("rd,fd->rf", upstream, back_down, preferred_element_type=jnp.float32)
    unused_value, gelu_pull = jax.vjp(gelu_tanh, hidden)
    hidden_grad = gelu_pull(active_grad)[0].astype(jnp.bfloat16)
    grad_heads = split_heads(attended_grad)
    sums_grouped = log_sums.reshape(seq_count, per_sequence, local_heads, block_rows)

    def backward_sequence(sequence):
        seq_ids = block_ids[sequence]
        seq_queries = queries[sequence]
        seq_keys = key_rows[sequence]
        seq_values = value_rows[sequence]
        seq_grads = grad_heads[sequence]
        seq_sums = sums_grouped[sequence]

        def backward_block(running, block_number):
            key_total, value_total = running
            offset = block_number * block_rows
            query_block = lax.dynamic_slice_in_dim(seq_queries, offset, block_rows, 0)
            query_ids = lax.dynamic_slice_in_dim(seq_ids, offset, block_rows, 0)
            grad_block = lax.dynamic_slice_in_dim(seq_grads, offset, block_rows, 0)
            scores = masked_scores(query_block, seq_keys, query_ids, seq_ids)
            prob_rows = jnp.exp(scores - seq_sums[block_number][:, :, None])
            value_total = value_total + jnp.einsum(
                "hqk,qhd->khd",
                prob_rows.astype(jnp.bfloat16),
                grad_block,
                preferred_element_type=jnp.float32,
            )
            prob_grad = jnp.einsum(
                "qhd,khd->hqk", grad_block, seq_values, preferred_element_type=jnp.float32
            )
            row_inner = jnp.sum(prob_grad * prob_rows, axis=2, keepdims=True)
            score_grad = (prob_rows * (prob_grad - row_inner)).astype(jnp.bfloat16)
            query_part = (
                jnp.einsum("hqk,khd->qhd", score_grad, seq_keys, preferred_element_type=jnp.float32)
                * score_scale
            )
            key_total = (
                key_total
                + jnp.einsum(
                    "hqk,qhd->khd", score_grad, query_block, preferred_element_type=jnp.float32
                )
                * score_scale
            )
            return ((key_total, value_total), query_part)

        zero_total = jnp.zeros((length, local_heads, HEAD_DIM), jnp.float32)
        (key_total, value_total), query_parts = lax.scan(
            backward_block, (zero_total, zero_total), jnp.arange(per_sequence)
        )
        return (query_parts.reshape(length, local_heads, HEAD_DIM), key_total, value_total)

    query_grad_rot, key_grad_rot, value_grad_all = lax.map(backward_sequence, jnp.arange(seq_count))
    query_grad = (
        rotate(query_grad_rot, cos_table, -sin_table)
        .reshape(all_rows, local_width)
        .astype(jnp.bfloat16)
    )
    key_grad = (
        rotate(key_grad_rot, cos_table, -sin_table)
        .reshape(all_rows, local_width)
        .astype(jnp.bfloat16)
    )
    value_grad = value_grad_all.reshape(all_rows, local_width).astype(jnp.bfloat16)
    query_wgrad = jnp.einsum("rd,rk->dk", back_rows, query_grad, preferred_element_type=jnp.float32)
    key_wgrad = jnp.einsum("rd,rk->dk", back_rows, key_grad, preferred_element_type=jnp.float32)
    value_wgrad = jnp.einsum("rd,rk->dk", back_rows, value_grad, preferred_element_type=jnp.float32)
    up_wgrad = jnp.einsum("rd,rf->df", back_rows, hidden_grad, preferred_element_type=jnp.float32)
    normed_grad = lax.psum_scatter(
        jnp.einsum("rk,dk->rd", query_grad, back_query, preferred_element_type=jnp.float32)
        + jnp.einsum("rk,dk->rd", key_grad, back_key, preferred_element_type=jnp.float32)
        + jnp.einsum("rk,dk->rd", value_grad, back_value, preferred_element_type=jnp.float32)
        + jnp.einsum("rf,df->rd", hidden_grad, back_up, preferred_element_type=jnp.float32),
        "tensor",
        scatter_dimension=0,
        tiled=True,
    )
    unused_norm, norm_pull = jax.vjp(normalize, inputs_float, gain_float, shift_float)
    input_part, gain_part, shift_part = norm_pull(normed_grad)
    input_grad = (grad_out.astype(jnp.float32) + input_part).astype(jnp.bfloat16)
    bias_part = jnp.sum(grad_out, axis=0, dtype=jnp.float32)
    gain_grad, shift_grad, outer_bias_grad = lax.psum(
        (gain_part, shift_part, bias_part), ("dp", "tensor")
    )
    query_bias_grad, key_bias_grad, value_bias_grad, up_bias_grad = lax.psum(
        (
            jnp.sum(query_grad, axis=0, dtype=jnp.float32),
            jnp.sum(key_grad, axis=0, dtype=jnp.float32),
            jnp.sum(value_grad, axis=0, dtype=jnp.float32),
            jnp.sum(hidden_grad, axis=0, dtype=jnp.float32),
        ),
        "dp",
    )
    (
        query_weight_grad,
        key_weight_grad,
        value_weight_grad,
        up_weight_grad,
        out_weight_grad,
        down_weight_grad,
    ) = (
        lax.psum_scatter(query_wgrad, "dp", scatter_dimension=0, tiled=True),
        lax.psum_scatter(key_wgrad, "dp", scatter_dimension=0, tiled=True),
        lax.psum_scatter(value_wgrad, "dp", scatter_dimension=0, tiled=True),
        lax.psum_scatter(up_wgrad, "dp", scatter_dimension=0, tiled=True),
        lax.psum_scatter(out_wgrad, "dp", scatter_dimension=1, tiled=True),
        lax.psum_scatter(down_wgrad, "dp", scatter_dimension=1, tiled=True),
    )
    return (
        output,
        input_grad,
        gain_grad,
        shift_grad,
        query_weight_grad,
        query_bias_grad,
        key_weight_grad,
        key_bias_grad,
        value_weight_grad,
        value_bias_grad,
        out_weight_grad,
        outer_bias_grad,
        up_weight_grad,
        up_bias_grad,
        down_weight_grad,
        outer_bias_grad,
    )


def solution(mesh):
    return jax.shard_map(
        per_device,
        mesh=mesh,
        in_specs=(
            P(("dp", "tensor"), None),
            P("dp", None),
            P(),
            P(),
            P("dp", "tensor"),
            P("tensor"),
            P("dp", "tensor"),
            P("tensor"),
            P("dp", "tensor"),
            P("tensor"),
            P("tensor", "dp"),
            P(),
            P("dp", "tensor"),
            P("tensor"),
            P("tensor", "dp"),
            P(),
            P(("dp", "tensor"), None),
        ),
        out_specs=(
            P(("dp", "tensor"), None),
            P(("dp", "tensor"), None),
            P(),
            P(),
            P("dp", "tensor"),
            P("tensor"),
            P("dp", "tensor"),
            P("tensor"),
            P("dp", "tensor"),
            P("tensor"),
            P("tensor", "dp"),
            P(),
            P("dp", "tensor"),
            P("tensor"),
            P("tensor", "dp"),
            P(),
        ),
        check_vma=False,
    )
```

profile of v0, /device:TPU:0, one launch (start us, length us, event | category | flops | bytes accessed | tf_op | source)
XLA Modules:
  0.0 2073.4 jit_solution(4787446761198307838)
XLA Ops:
  22.7 16.5 all-gather.15.cloned.1.call-done
  39.2 153.3 %all-gather.9.cloned.1.call-done = bf16[4096,2048]{1,0:T(8,128)(2,1)} async-done(((bf16[512,2048]{1,0:T(8,128)(2,1)}), bf16[4096,2048]{1,0:T(8,128)(2,1)}) %all-gather.9.cloned.1.call-update) | async-done | bytes 16777232 | tf_op jit(solution)/shard_map/all_gather | solution.py:87
  192.5 12.6 convolution_add_fusion.1
  222.3 12.6 convolution_add_fusion.2
  252.4 12.1 fusion.53
  264.6 7.1 reshape.277
  278.6 149.8 %all-gather.23.cloned.1.call-done = bf16[4096,2048]{1,0:T(8,128)(2,1)} async-done(((bf16[512,2048]{1,0:T(8,128)(2,1)}), bf16[4096,2048]{1,0:T(8,128)(2,1)}) %all-gather.23.cloned.1.call-update) | async-done | bytes 16777232 | tf_op jit(solution)/shard_map/all_gather | solution.py:145
  428.4 11.9 convolution_convert_fusion
  440.3 7.4 reshape.276
  447.8 7.0 copy.63
  466.2 102.8 %while.44 = (s32[]{:T(128)}, bf16[8,512,4,64]{1,3,2,0:T(8,128)(2,1)S(1)}, f32[8,4,512]{2,1,0:T(4,128)S(1)}, s32[8]{0:T(128)S(1)}, bf16[4,1024,4,64]{1,3,2,0:T(8,...) while((s32[]{:T(128)}, ...), condition=%wide.region_5.6_spmd, body=%wide.region_2.5_spmd.sunk | while | flops 562558976 | bytes 29182452 | solution.py:122
  570.3 342.7 %while.46 = (s32[]{:T(128)}, f32[4,1024,4,64]{1,0,3,2:T(4,128)}, f32[4,1024,4,64]{1,0,3,2:T(4,128)}, bf16[4,1024,4,64]{1,3,2,0:T(8,128)(2,1)}, s32[4]{0:T(128)S(...) while((s32[]{:T(128)}, f32[4,1024,4,64]{1,0,3,2:T(4,128)}, ...), condition=%wide.region_11.12_spmd, body=%wide.region_7.11_spmd.sunk | while | flops 1375598592 | bytes 110209856 | solution.py:203
  575.7 33.3 %while.47 = (s32[]{:T(128)}, f32[1024,4,64]{0,2,1:T(8,128)S(1)}, f32[1024,4,64]{0,2,1:T(8,128)}, f32[2,512,4,64]{1,3,2,0:T(8,128)}, s32[2]{0:T(128)S(1)}, /*inde...) while((s32[]{:T(128)}, f32[1024,4,64]{0,2,1:T(8,128)S(1)}, ...), condition=%wide.region_10.10_spmd.clone, body=%wide.region_8.9_spmd.clone.sunk | while | flops 1375598592 | bytes 89196952 | solution.py:198
  616.2 19.9 dynamic_update_slice.44
  636.1 19.9 dynamic_update_slice.45
  661.3 33.3 %while.47 = (s32[]{:T(128)}, f32[1024,4,64]{0,2,1:T(8,128)S(1)}, f32[1024,4,64]{0,2,1:T(8,128)}, f32[2,512,4,64]{1,3,2,0:T(8,128)}, s32[2]{0:T(128)S(1)}, /*inde...) while((s32[]{:T(128)}, f32[1024,4,64]{0,2,1:T(8,128)S(1)}, ...), condition=%wide.region_10.10_spmd.clone, body=%wide.region_8.9_spmd.clone.sunk | while | flops 1375598592 | bytes 89196952 | solution.py:198
  701.8 19.9 dynamic_update_slice.44
  721.7 19.9 dynamic_update_slice.45
  746.9 33.3 %while.47 = (s32[]{:T(128)}, f32[1024,4,64]{0,2,1:T(8,128)S(1)}, f32[1024,4,64]{0,2,1:T(8,128)}, f32[2,512,4,64]{1,3,2,0:T(8,128)}, s32[2]{0:T(128)S(1)}, /*inde...) while((s32[]{:T(128)}, f32[1024,4,64]{0,2,1:T(8,128)S(1)}, ...), condition=%wide.region_10.10_spmd.clone, body=%wide.region_8.9_spmd.clone.sunk | while | flops 1375598592 | bytes 89196952 | solution.py:198
  787.4 19.9 dynamic_update_slice.44
  807.3 19.9 dynamic_update_slice.45
  832.5 33.3 %while.47 = (s32[]{:T(128)}, f32[1024,4,64]{0,2,1:T(8,128)S(1)}, f32[1024,4,64]{0,2,1:T(8,128)}, f32[2,512,4,64]{1,3,2,0:T(8,128)}, s32[2]{0:T(128)S(1)}, /*inde...) while((s32[]{:T(128)}, f32[1024,4,64]{0,2,1:T(8,128)S(1)}, ...), condition=%wide.region_10.10_spmd.clone, body=%wide.region_8.9_spmd.clone.sunk | while | flops 1375598592 | bytes 89196952 | solution.py:198
  873.0 19.9 dynamic_update_slice.44
  892.9 19.9 dynamic_update_slice.45
  929.1 13.1 fusion.81
  942.3 13.5 fusion.82
  959.7 13.1 fusion.83
  972.8 23.4 %fusion.80 = f32[4096,1024]{1,0:T(8,128)} fusion(bf16[4096,2048]{1,0:T(8,128)(2,1)} %all-gather.9.cloned.1.call-done, bf16[2048,1024]{1,0:T(8,128)(2,1)} %all-gather.19.cloned.1.call-done), kind=kOutput, calls=%fused_computation.136 | convolution fusion | flops 17179869184 | bytes 37748736 | tf_op jit(solution)/shard_map/dot_general | solution.py:91
  996.2 36.5 %convert_reduce_fusion = (f32[1024]{0:T(1024)}, bf16[4096,1024]{1,0:T(8,128)(2,1)}) fusion(f32[4096,1024]{1,0:T(8,128)} %fusion.80, f32[1024]{0:T(1024)S(1)} %copy-done.40, bf16[4096,2048]{1,0:T(8,128)(2,1)} %all-gather.23.cloned.1.call-done, bf16[1024,2048]{1,0:T(8,128)(2,1)} %all-gather.21.cloned.1.call-done), kind=kOutput, calls=%fused_computation.68 | convolution fusion | flops 17276338176 | bytes 46145536 | tf_op jit(solution)/shard_map/rd,fd->rf/dot_general | solution.py:151
  1032.6 48.6 %add_add_fusion = f32[4096,2048]{1,0:T(8,128)} fusion(f32[4096,2048]{1,0:T(8,128)} %fusion.83, f32[4096,2048]{1,0:T(8,128)} %fusion.81, f32[4096,2048]{1,0:T(8,128)} %fusion.82, bf16[4096,1024]{1,0:T(8,128)(2,1)} %get-tuple-element.433, bf16[2048,1024]{1,0:T(8,128)(2,1)} %all-gather.19.cloned.1.call-done), kind=kOutput, calls=%fused_computation.57 | convolution fusion | flops 17205035008 | bytes 146800640 | tf_op jit(solution)/shard_map/rf,df->rd/dot_general | solution.py:223
  1086.3 13.4 fusion.79
  1099.7 34.0 %convolution_add_fusion = f32[4096,2048]{1,0:T(8,128)} fusion(f32[4096,2048]{1,0:T(8,128)} %fusion.79, bf16[1024,2048]{1,0:T(8,128)(2,1)S(1)} %copy-done.42, f32[4096,1024]{1,0:T(8,128)} %fusion.80, f32[1024]{0:T(1024)S(1)} %copy-done.40), kind=kOutput, calls=%fused_computation.60 | convolution fusion | flops 17230200832 | bytes 88084480 | tf_op jit(solution)/shard_map/dot_general | solution.py:128
  1133.7 12.5 fusion.87
  1146.8 9.8 fusion.86
  1156.7 13.1 fusion.85
  1169.8 9.8 fusion.84
  1179.9 24.2 %fusion.88 = f32[2048,1024]{1,0:T(8,128)} fusion(bf16[4096,2048]{1,0:T(8,128)(2,1)} %all-gather.9.cloned.1.call-done, bf16[4096,1024]{1,0:T(8,128)(2,1)} %get-tuple-element.433), kind=kOutput, calls=%fused_computation.144 | convolution fusion | flops 17179869184 | bytes 33554432 | tf_op jit(solution)/shard_map/rd,rf->df/dot_general | solution.py:218
  1204.2 28.9 %fusion.76 = f32[1024,2048]{1,0:T(8,128)} fusion(bf16[4096,2048]{1,0:T(8,128)(2,1)} %all-gather.23.cloned.1.call-done, f32[4096,1024]{1,0:T(8,128)} %fusion.80, f32[1024]{0:T(1024)S(1)} %copy-done.40), kind=kOutput, calls=%fused_computation.133 | convolution fusion | flops 17221812224 | bytes 41947136 | tf_op jit(solution)/shard_map/rf,rd->fd/dot_general | solution.py:147
  1236.1 10.8 all-reduce.1
  1246.9 158.2 %reduce-scatter.11.cloned.1.call-done = f32[512,2048]{1,0:T(8,128)} async-done(((f32[4096,2048]{1,0:T(8,128)}), f32[512,2048]{1,0:T(8,128)}) %reduce-scatter.11.cloned.1.call-update) | async-done | bytes 4194320 | tf_op jit(solution)/shard_map/reduce_scatter | solution.py:219
  1410.6 320.8 %reduce-scatter.9.cloned.1.call-done = f32[512,2048]{1,0:T(8,128)} async-done(((f32[4096,2048]{1,0:T(8,128)}), f32[512,2048]{1,0:T(8,128)}) %reduce-scatter.9.cloned.1.call-update) | async-done | bytes 4194320 | tf_op jit(solution)/shard_map/reduce_scatter | solution.py:126
  1731.4 7.6 convert_reduce_fusion.2
  1739.0 38.3 %all-reduce = (f32[2048]{0:T(1024)}, f32[2048]{0:T(1024)}, f32[2048]{0:T(1024)S(1)}) all-reduce(f32[2048]{0:T(1024)S(1)} %get-tuple-element.359, f32[2048]{0:T(1024)S(1)} %get-tuple-element.361, f32[2048]{0:T(1024)S(1)} %get-tuple-element.458), channel_id=1, replica_groups=mesh['dp'=4,'tensor'=8] {'dp','tensor'}, use_global_device_ids=true, to_apply=%region_16.17 | all-reduce | flops 6144 | bytes 49152 | tf_op jit(solution)/shard_map/psum | solution.py:232
  1777.3 30.9 %reduce-scatter.17.cloned.1.call-done = f32[512,256]{1,0:T(8,128)} async-done(((f32[2048,256]{1,0:T(8,128)}), f32[512,256]{1,0:T(8,128)}) %reduce-scatter.17.cloned.1.call-update) | async-done | bytes 524304 | tf_op jit(solution)/shard_map/reduce_scatter | solution.py:254
  1808.2 38.7 %reduce-scatter.15.cloned.1.call-done = f32[512,256]{1,0:T(8,128)} async-done(((f32[2048,256]{1,0:T(8,128)}), f32[512,256]{1,0:T(8,128)}) %reduce-scatter.15.cloned.1.call-update) | async-done | bytes 524304 | tf_op jit(solution)/shard_map/reduce_scatter | solution.py:253
  1847.0 38.9 %reduce-scatter.13.cloned.1.call-done = f32[512,256]{1,0:T(8,128)} async-done(((f32[2048,256]{1,0:T(8,128)}), f32[512,256]{1,0:T(8,128)}) %reduce-scatter.13.cloned.1.call-update) | async-done | bytes 524304 | tf_op jit(solution)/shard_map/reduce_scatter | solution.py:252
  1885.9 89.9 %reduce-scatter.21.cloned.1.call-done = f32[512,1024]{1,0:T(8,128)} async-done(((f32[2048,1024]{1,0:T(8,128)}), f32[512,1024]{1,0:T(8,128)}) %reduce-scatter.21.cloned.1.call-update) | async-done | bytes 2097168 | tf_op jit(solution)/shard_map/reduce_scatter | solution.py:255
  1975.8 90.2 %reduce-scatter.23.cloned.1.call-done = f32[1024,512]{1,0:T(8,128)} async-done(((f32[1024,2048]{1,0:T(8,128)}), f32[1024,512]{1,0:T(8,128)}) %reduce-scatter.23.cloned.1.call-update) | async-done | bytes 2097168 | tf_op jit(solution)/shard_map/reduce_scatter | solution.py:257
  (444 shorter events, 339.3 us)
Async XLA Ops:
  7.2 7.6 copy-start.1
  7.2 32.0 %all-gather.15.cloned.1.call-start = ((), (), s32[]{:S(2)}) async-start(), calls=%async_computation.11 | async-start | bytes 1310720 | tf_op jit(solution)/shard_map/all_gather | solution.py:81
  7.9 184.6 %all-gather.9.cloned.1.call-start = ((), (), s32[]{:S(2)}) async-start(), calls=%async_computation.8 | async-start | bytes 18874368 | tf_op jit(solution)/shard_map/all_gather | solution.py:87
  8.7 5.5 copy-start.25
  16.9 4.1 copy-start.43
  16.9 4.1 copy-start.44
  16.9 4.2 copy-start.45
  16.9 4.2 copy-start.41
  17.0 205.3 %all-gather.13.cloned.1.call-start = ((), (), s32[]{:S(2)}) async-start(), calls=%async_computation.10 | async-start | bytes 1310720 | tf_op jit(solution)/shard_map/all_gather | solution.py:80
  17.7 234.8 %all-gather.11.cloned.1.call-start = ((), (), s32[]{:S(2)}) async-start(), calls=%async_computation.9 | async-start | bytes 1310720 | tf_op jit(solution)/shard_map/all_gather | solution.py:82
  18.3 260.3 %all-gather.17.cloned.1.call-start = ((), (), s32[]{:S(2)}) async-start(), calls=%async_computation.12 | async-start | bytes 1310720 | tf_op jit(solution)/shard_map/all_gather | solution.py:84
  18.9 409.6 %all-gather.23.cloned.1.call-start = ((), (), s32[]{:S(2)}) async-start(), calls=%async_computation.16 | async-start | bytes 18874368 | tf_op jit(solution)/shard_map/all_gather | solution.py:145
  19.4 953.3 %all-gather.19.cloned.1.call-start = ((), (), s32[]{:S(2)}) async-start(), calls=%async_computation.13 | async-start | bytes 5242880 | tf_op jit(solution)/shard_map/all_gather | solution.py:83
  20.2 976.0 %all-gather.21.cloned.1.call-start = ((), (), s32[]{:S(2)}) async-start(), calls=%async_computation.14 | async-start | bytes 5242880 | tf_op jit(solution)/shard_map/all_gather | solution.py:85
  20.9 1384.2 %reduce-scatter.11.cloned.1.call-start = ((), (), s32[]{:S(2)}) async-start(), calls=%async_computation.17 | async-start | bytes 37748736 | tf_op jit(solution)/shard_map/reduce_scatter | solution.py:219
  22.7 432.1 %copy-start.20 = (f32[1024,32]{0,1:T(8,128)}, f32[1024,32]{0,1:T(8,128)S(1)}, u32[]{:S(2)}) copy-start(f32[1024,32]{0,1:T(8,128)S(1)} %get-tuple-element.467) | copy-start | bytes 393220
  462.2 4.0 copy-start.17
  462.3 4.0 copy-start.27
  614.1 22.1 %copy-start = (f32[1,1024,4,64]{1,0,3,2:T(1,128)S(1)}, f32[1,1024,4,64]{1,0,3,2:T(1,128)}, u32[]{:S(2)}) copy-start(f32[1,1024,4,64]{1,0,3,2:T(1,128)} %copy.103) | copy-start | bytes 3145732 | tf_op jit(solution)/shard_map/while
  699.6 22.1 %copy-start = (f32[1,1024,4,64]{1,0,3,2:T(1,128)S(1)}, f32[1,1024,4,64]{1,0,3,2:T(1,128)}, u32[]{:S(2)}) copy-start(f32[1,1024,4,64]{1,0,3,2:T(1,128)} %copy.103) | copy-start | bytes 3145732 | tf_op jit(solution)/shard_map/while
  785.2 22.1 %copy-start = (f32[1,1024,4,64]{1,0,3,2:T(1,128)S(1)}, f32[1,1024,4,64]{1,0,3,2:T(1,128)}, u32[]{:S(2)}) copy-start(f32[1,1024,4,64]{1,0,3,2:T(1,128)} %copy.103) | copy-start | bytes 3145732 | tf_op jit(solution)/shard_map/while
  870.8 22.1 %copy-start = (f32[1,1024,4,64]{1,0,3,2:T(1,128)S(1)}, f32[1,1024,4,64]{1,0,3,2:T(1,128)}, u32[]{:S(2)}) copy-start(f32[1,1024,4,64]{1,0,3,2:T(1,128)} %copy.103) | copy-start | bytes 3145732 | tf_op jit(solution)/shard_map/while
  913.0 4.1 copy-start.16
  925.2 17.1 copy-start.10
  925.2 3.9 copy-start.23
  929.1 13.2 copy-start.8
  929.1 13.2 copy-start.21
  942.3 13.6 copy-start.14
  955.8 3.9 copy-start.24
  972.8 23.4 %copy-start.40 = (f32[1024]{0:T(1024)S(1)}, f32[1024]{0:T(1024)}, u32[]{:S(2)}) copy-start(f32[1024]{0:T(1024)} %convert_element_type.123) | copy-start | bytes 12292
  1081.3 650.1 %reduce-scatter.9.cloned.1.call-start = ((), (), s32[]{:S(2)}) async-start(), calls=%async_computation.15 | async-start | bytes 37748736 | tf_op jit(solution)/shard_map/reduce_scatter | solution.py:126
  1082.9 3.4 copy-start.22
  1086.3 13.4 copy-start.42
  1133.7 13.1 copy-start.12
  1133.7 643.6 %reduce-scatter.19.cloned.1.call-start = ((), (), s32[]{:S(2)}) async-start(), calls=%async_computation.21 | async-start | bytes 2621440 | tf_op jit(solution)/shard_map/reduce_scatter | solution.py:256
  1146.3 661.9 %reduce-scatter.17.cloned.1.call-start = ((), (), s32[]{:S(2)}) async-start(), calls=%async_computation.20 | async-start | bytes 2621440 | tf_op jit(solution)/shard_map/reduce_scatter | solution.py:254
  1156.6 13.2 copy-start.9
  1156.6 690.4 %reduce-scatter.15.cloned.1.call-start = ((), (), s32[]{:S(2)}) async-start(), calls=%async_computation.19 | async-start | bytes 2621440 | tf_op jit(solution)/shard_map/reduce_scatter | solution.py:253
  1169.7 716.2 %reduce-scatter.13.cloned.1.call-start = ((), (), s32[]{:S(2)}) async-start(), calls=%async_computation.18 | async-start | bytes 2621440 | tf_op jit(solution)/shard_map/reduce_scatter | solution.py:252
  1179.7 796.2 %reduce-scatter.21.cloned.1.call-start = ((), (), s32[]{:S(2)}) async-start(), calls=%async_computation.22 | async-start | bytes 10485760 | tf_op jit(solution)/shard_map/reduce_scatter | solution.py:255
  1204.2 861.9 %reduce-scatter.23.cloned.1.call-start = ((), (), s32[]{:S(2)}) async-start(), calls=%async_computation.23 | async-start | bytes 10485760 | tf_op jit(solution)/shard_map/reduce_scatter | solution.py:257
  1233.1 172.1 %copy-start.2 = (bf16[512,2048]{1,0:T(8,128)(2,1)S(1)}, bf16[512,2048]{1,0:T(8,128)(2,1)}, u32[]{:S(2)}) copy-start(bf16[512,2048]{1,0:T(8,128)(2,1)} %param.23) | copy-start | bytes 6291460
  1233.1 172.0 %copy-start.26 = (f32[2048]{0:T(1024)S(1)}, f32[2048]{0:T(1024)}, u32[]{:S(2)}) copy-start(f32[2048]{0:T(1024)} %copy-done.25) | copy-start | bytes 24580
  1233.1 172.0 %copy-start.29 = (f32[512]{0:T(512)S(1)}, f32[512]{0:T(512)}, u32[]{:S(2)}) copy-start(f32[512]{0:T(512)} %copy-done.28) | copy-start | bytes 6148
  1233.8 174.7 %copy-start.33 = (f32[512]{0:T(512)S(1)}, f32[512]{0:T(512)}, u32[]{:S(2)}) copy-start(f32[512]{0:T(512)} %copy-done.32) | copy-start | bytes 6148
  1233.8 174.7 %copy-start.31 = (f32[512]{0:T(512)S(1)}, f32[512]{0:T(512)}, u32[]{:S(2)}) copy-start(f32[512]{0:T(512)} %copy-done.30) | copy-start | bytes 6148
  1405.1 3.5 copy-start.3
  1777.3 289.3 %copy-start.36 = (f32[2048]{0:T(1024)}, f32[2048]{0:T(1024)S(1)}, u32[]{:S(2)}) copy-start(f32[2048]{0:T(1024)S(1)} %get-tuple-element.893) | copy-start | bytes 24580
  (45 other events, 76.2 us)
Sparse Core Ops, SparseCore 0:
  9.9 29.3 all-gather.14
  41.4 151.0 all-gather.8
  194.4 24.8 all-gather.12
  221.0 26.6 all-gather.10
  249.3 26.4 all-gather.16
  277.3 151.1 all-gather.22
  430.3 50.9 all-gather.18
  483.1 52.5 all-gather.20
  1081.4 323.6 reduce-scatter.10
  1407.5 323.8 reduce-scatter.8
  1735.0 34.3 reduce-scatter.18
  1773.0 35.1 reduce-scatter.16
  1811.8 35.1 reduce-scatter.14
  1850.7 35.2 reduce-scatter.12
  1889.4 86.3 reduce-scatter.20
  1979.6 86.3 reduce-scatter.22
where the time goes:
time: 2090 us; the launch traced here: 2070 us
  waiting for transfers between devices  1090 us (52%)
  matrix products  473 us (23%)
  local copies, waits for them, and re-layouts  297 us (14%)
  other arithmetic  95.4 us (5%)
  loops' own time  51.3 us (2%)
  blocking collectives  49.1 us (2%)
    reduce_scatter x1, waiting for transfers between devices, per_device(): lax.psum_scatter(jnp.dot(attended_low, full_out, preferred_element_type=j...  321 us
    dynamic_update_slice x20, local copies, waits for them, and re-layouts, per_device(): lax.map(backward_sequence, jnp.arange(seq_count))  181 us
    reduce_scatter x1, waiting for transfers between devices, per_device(): lax.psum_scatter(jnp.einsum('rk,dk->rd', query_grad, back_query, preferre...  158 us
    all_gather x1, waiting for transfers between devices, per_device(): group_rows = lax.all_gather(normed, 'tensor', axis=0, tiled=True)  153 us
    all_gather x1, waiting for transfers between devices, per_device(): upstream = lax.all_gather(grad_out, 'tensor', axis=0, tiled=True)  150 us
    reduce_scatter x1, waiting for transfers between devices, per_device(): lax.psum_scatter(down_wgrad, 'dp', scatter_dimension=1, tiled=True)  90.2 us
    reduce_scatter x1, waiting for transfers between devices, per_device(): lax.psum_scatter(up_wgrad, 'dp', scatter_dimension=0, tiled=True)  89.9 us
    dot_general x4, matrix products, project(): jnp.dot(group_rows, weight_part, preferred_element_type=jnp.float32)  60.7 us
  transfers between devices with their start and end apart: 16, of which 10 were waited for; matrix products, arithmetic and copies ran while one was open for 37% of the time, Pallas kernels for 0%

commit v1 on v0

--- a/solution.py
+++ b/solution.py
@@ -6,6 +6,24 @@
 HEAD_DIM = 64
 ROT = 32
 eps_norm = 1e-05
+
+
+def ring_gather(array, axis, dim):
+    ways, here, lap = (lax.axis_size(axis), lax.axis_index(axis), array.shape[dim])
+    shape = [n * ways if d == dim else n for d, n in enumerate(array.shape)]
+    full = lax.dynamic_update_slice_in_dim(
+        jnp.zeros(shape, array.dtype), array, here * lap, axis=dim
+    )
+    going_up = going_down = array
+    for far in range(1, ways // 2 + 1):
+        going_up = lax.ppermute(going_up, axis, [(d, (d + 1) % ways) for d in range(ways)])
+        full = lax.dynamic_update_slice_in_dim(full, going_up, (here - far) % ways * lap, axis=dim)
+        if 2 * far < ways:
+            going_down = lax.ppermute(going_down, axis, [(d, (d - 1) % ways) for d in range(ways)])
+            full = lax.dynamic_update_slice_in_dim(
+                full, going_down, (here + far) % ways * lap, axis=dim
+            )
+    return full
 
 
 def normalize(values, gain_in, shift_in):
@@ -84,7 +102,7 @@
         lax.all_gather(out_weight, "dp", axis=1, tiled=True),
         lax.all_gather(down_weight, "dp", axis=1, tiled=True),
     )
-    group_rows = lax.all_gather(normed, "tensor", axis=0, tiled=True)
+    group_rows = ring_gather(normed, "tensor", 0)
     cos_table, sin_table = rotary_tables(length, ROT)
 
     def project(weight_part, bias_part):

time: 2090 us -> 1960 us (0.938)
  waiting for transfers between devices: 1090 us -> 935 us
  local copies, waits for them, and re-layouts: 297 us -> 320 us
    all_gather x1, waiting for transfers between devices: 153 us -> 0.02 us  [per_device(): back_rows = lax.all_gather(normed, 'tensor', axis=0, tiled=True)]
    all_gather x1, waiting for transfers between devices: 150 us -> 0.01 us  [per_device(): upstream = lax.all_gather(grad_out, 'tensor', axis=0, tiled=True)]
    ppermute x0 -> x7, waiting for transfers between devices: none -> 137 us  [the longest x4 136 us: ring_gather(): lax.ppermute(going_up, axis, [(d, (d + 1) % ways) for d in range(ways)])]
    reduce_scatter x1, waiting for transfers between devices: 30.9 us -> 0.02 us  [per_device(): lax.psum_scatter(value_wgrad, 'dp', scatter_dimension=0, tiled=True)]
    reduce_scatter x1, waiting for transfers between devices: 0.02 us -> 30.9 us  [per_device(): lax.psum_scatter(out_wgrad, 'dp', scatter_dimension=1, tiled=True)]
    reduce_scatter x1, waiting for transfers between devices: 158 us -> 184 us  [per_device(): lax.psum_scatter(jnp.einsum('rk,dk->rd', query_grad, back_query, preferre...]
  transfers between devices with their start and end apart: 16 -> 23, of which waited for: 10 -> 13; matrix products, arithmetic and copies ran while one was open for 37% -> 44% of each run, Pallas kernels for 0% -> 0%
where the time goes in v1:
time: 1960 us; the launch traced here: 1950 us
  waiting for transfers between devices  935 us (48%)
  matrix products  472 us (24%)
  local copies, waits for them, and re-layouts  320 us (16%)
  other arithmetic  87.6 us (4%)
  blocking collectives  53.6 us (3%)
  loops' own time  51.6 us (3%)
    reduce_scatter x1, waiting for transfers between devices, per_device(): lax.psum_scatter(jnp.dot(attended_low, full_out, preferred_element_type=j...  321 us
    reduce_scatter x1, waiting for transfers between devices, per_device(): lax.psum_scatter(jnp.einsum('rk,dk->rd', query_grad, back_query, preferre...  184 us
    dynamic_update_slice x20, local copies, waits for them, and re-layouts, per_device(): lax.map(backward_sequence, jnp.arange(seq_count))  181 us
    ppermute x4, waiting for transfers between devices, ring_gather(): lax.ppermute(going_up, axis, [(d, (d + 1) % ways) for d in range(ways)])  136 us
    reduce_scatter x1, waiting for transfers between devices, per_device(): lax.psum_scatter(down_wgrad, 'dp', scatter_dimension=1, tiled=True)  90.2 us
    reduce_scatter x1, waiting for transfers between devices, per_device(): lax.psum_scatter(up_wgrad, 'dp', scatter_dimension=0, tiled=True)  89.9 us
    dot_general x4, matrix products, project(): jnp.dot(group_rows, weight_part, preferred_element_type=jnp.float32)  62.1 us
    dot_general x1, matrix products, per_device(): jnp.einsum('rf,df->rd', hidden_grad, back_up, preferred_element_type=jnp....  48.7 us
  transfers between devices with their start and end apart: 23, of which 13 were waited for; matrix products, arithmetic and copies ran while one was open for 44% of the time, Pallas kernels for 0%

profile of v1, /device:TPU:0, one launch (start us, length us, event | category | flops | bytes accessed | tf_op | source)
XLA Modules:
  0.0 1948.4 jit_solution(48368167901641121)
XLA Ops:
  28.3 43.7 %collective-permute-done = bf16[512,2048]{1,0:T(8,128)(2,1)S(1)} collective-permute-done((bf16[512,2048]{1,0:T(8,128)(2,1)}, bf16[512,2048]{1,0:T(8,128)(2,1)S(1)}, u32[]{:S(2)}, u32[]{:S(2)}) %collective-permute-start) | collective-permute-done | bytes 2097184 | tf_op jit(solution)/shard_map/ppermute | solution.py:19
  76.3 42.0 %collective-permute-done.2 = bf16[512,2048]{1,0:T(8,128)(2,1)} collective-permute-done((bf16[512,2048]{1,0:T(8,128)(2,1)S(1)}, bf16[512,2048]{1,0:T(8,128)(2,1)}, u32[]{:S(2)}, u32[]{:S(2)}) %collective-permute-start.2) | collective-permute-done | bytes 2097184 | tf_op jit(solution)/shard_map/ppermute | solution.py:19
  123.9 39.2 %collective-permute-done.4 = bf16[512,2048]{1,0:T(8,128)(2,1)} collective-permute-done((bf16[512,2048]{1,0:T(8,128)(2,1)}, bf16[512,2048]{1,0:T(8,128)(2,1)}, u32[]{:S(2)}, u32[]{:S(2)}) %collective-permute-start.4) | collective-permute-done | bytes 2097184 | tf_op jit(solution)/shard_map/ppermute | solution.py:19
  179.9 10.9 collective-permute-done.6
  192.3 13.1 convolution_add_fusion.1
  222.7 12.6 convolution_add_fusion.2
  253.1 12.1 fusion.53
  265.2 7.1 reshape.277
  272.3 7.0 copy.55
  290.1 103.0 %while.44 = (s32[]{:T(128)}, bf16[8,512,4,64]{1,3,2,0:T(8,128)(2,1)S(1)}, f32[8,4,512]{2,1,0:T(4,128)S(1)}, s32[8]{0:T(128)S(1)}, bf16[4,1024,4,64]{1,3,2,0:T(8,...) while((s32[]{:T(128)}, ...), condition=%wide.region_5.6_spmd, body=%wide.region_2.5_spmd.sunk | while | flops 562558976 | bytes 29182452 | solution.py:140
  393.1 24.4 %fusion.81 = f32[4096,1024]{1,0:T(8,128)} fusion(bf16[4096,2048]{1,0:T(8,128)(2,1)} %constant_dynamic-update-slice_fusion, bf16[2048,1024]{1,0:T(8,128)(2,1)} %all-gather.17.cloned.1.call-done), kind=kOutput, calls=%fused_computation.144 | convolution fusion | flops 17179869184 | bytes 37748736 | tf_op jit(solution)/shard_map/dot_general | solution.py:109
  417.5 10.8 convolution_convert_fusion
  438.5 343.9 %while.46 = (s32[]{:T(128)}, f32[4,1024,4,64]{1,0,3,2:T(4,128)}, f32[4,1024,4,64]{1,0,3,2:T(4,128)}, bf16[4,1024,4,64]{1,3,2,0:T(8,128)(2,1)}, s32[4]{0:T(128)S(...) while((s32[]{:T(128)}, f32[4,1024,4,64]{1,0,3,2:T(4,128)}, ...), condition=%wide.region_11.12_spmd, body=%wide.region_7.11_spmd.sunk | while | flops 1375598592 | bytes 110209856 | solution.py:221
  444.2 33.4 %while.47 = (s32[]{:T(128)}, f32[1024,4,64]{0,2,1:T(8,128)S(1)}, f32[1024,4,64]{0,2,1:T(8,128)}, f32[2,512,4,64]{1,3,2,0:T(8,128)}, s32[2]{0:T(128)S(1)}, /*inde...) while((s32[]{:T(128)}, f32[1024,4,64]{0,2,1:T(8,128)S(1)}, ...), condition=%wide.region_10.10_spmd.clone, body=%wide.region_8.9_spmd.clone.sunk | while | flops 1375598592 | bytes 89196952 | solution.py:216
  484.8 20.0 %dynamic_update_slice.84 = f32[4,1024,4,64]{1,0,3,2:T(4,128)} dynamic-update-slice(f32[4,1024,4,64]{1,0,3,2:T(4,128)} %get-tuple-element.827, f32[1,1024,4,64]{1,0,3,2:T(1,128)S(1)} %copy.102, s32[]{:T(128)S(6)} %copy.143, s32[]{:T(128)} %constant.263.clone.1..sunk.1, s32[]{:T(128)} %constant.263.clone.1..sunk.1, s32[]{:T(128)} %constant.263.clone.1..sunk.1) | dynamic-update-slice | bytes 2097156 | tf_op jit(solution)/shard_map/while/body/jit(dynamic_update_index_in_dim)/dynamic_update_slice | solution.py:221
  504.8 20.0 %dynamic_update_slice.85 = f32[4,1024,4,64]{1,0,3,2:T(4,128)} dynamic-update-slice(f32[4,1024,4,64]{1,0,3,2:T(4,128)} %get-tuple-element.828, f32[1,1024,4,64]{1,0,3,2:T(1,128)S(1)} %copy-done, s32[]{:T(128)S(6)} %copy.143, s32[]{:T(128)} %constant.263.clone.1..sunk.1, s32[]{:T(128)} %constant.263.clone.1..sunk.1, s32[]{:T(128)} %constant.263.clone.1..sunk.1) | dynamic-update-slice | bytes 2097156 | tf_op jit(solution)/shard_map/while/body/jit(dynamic_update_index_in_dim)/dynamic_update_slice | solution.py:221
  530.2 33.4 %while.47 = (s32[]{:T(128)}, f32[1024,4,64]{0,2,1:T(8,128)S(1)}, f32[1024,4,64]{0,2,1:T(8,128)}, f32[2,512,4,64]{1,3,2,0:T(8,128)}, s32[2]{0:T(128)S(1)}, /*inde...) while((s32[]{:T(128)}, f32[1024,4,64]{0,2,1:T(8,128)S(1)}, ...), condition=%wide.region_10.10_spmd.clone, body=%wide.region_8.9_spmd.clone.sunk | while | flops 1375598592 | bytes 89196952 | solution.py:216
  570.8 19.9 %dynamic_update_slice.84 = f32[4,1024,4,64]{1,0,3,2:T(4,128)} dynamic-update-slice(f32[4,1024,4,64]{1,0,3,2:T(4,128)} %get-tuple-element.827, f32[1,1024,4,64]{1,0,3,2:T(1,128)S(1)} %copy.102, s32[]{:T(128)S(6)} %copy.143, s32[]{:T(128)} %constant.263.clone.1..sunk.1, s32[]{:T(128)} %constant.263.clone.1..sunk.1, s32[]{:T(128)} %constant.263.clone.1..sunk.1) | dynamic-update-slice | bytes 2097156 | tf_op jit(solution)/shard_map/while/body/jit(dynamic_update_index_in_dim)/dynamic_update_slice | solution.py:221
  590.7 20.0 %dynamic_update_slice.85 = f32[4,1024,4,64]{1,0,3,2:T(4,128)} dynamic-update-slice(f32[4,1024,4,64]{1,0,3,2:T(4,128)} %get-tuple-element.828, f32[1,1024,4,64]{1,0,3,2:T(1,128)S(1)} %copy-done, s32[]{:T(128)S(6)} %copy.143, s32[]{:T(128)} %constant.263.clone.1..sunk.1, s32[]{:T(128)} %constant.263.clone.1..sunk.1, s32[]{:T(128)} %constant.263.clone.1..sunk.1) | dynamic-update-slice | bytes 2097156 | tf_op jit(solution)/shard_map/while/body/jit(dynamic_update_index_in_dim)/dynamic_update_slice | solution.py:221
  615.9 33.4 %while.47 = (s32[]{:T(128)}, f32[1024,4,64]{0,2,1:T(8,128)S(1)}, f32[1024,4,64]{0,2,1:T(8,128)}, f32[2,512,4,64]{1,3,2,0:T(8,128)}, s32[2]{0:T(128)S(1)}, /*inde...) while((s32[]{:T(128)}, f32[1024,4,64]{0,2,1:T(8,128)S(1)}, ...), condition=%wide.region_10.10_spmd.clone, body=%wide.region_8.9_spmd.clone.sunk | while | flops 1375598592 | bytes 89196952 | solution.py:216
  656.6 19.9 %dynamic_update_slice.84 = f32[4,1024,4,64]{1,0,3,2:T(4,128)} dynamic-update-slice(f32[4,1024,4,64]{1,0,3,2:T(4,128)} %get-tuple-element.827, f32[1,1024,4,64]{1,0,3,2:T(1,128)S(1)} %copy.102, s32[]{:T(128)S(6)} %copy.143, s32[]{:T(128)} %constant.263.clone.1..sunk.1, s32[]{:T(128)} %constant.263.clone.1..sunk.1, s32[]{:T(128)} %constant.263.clone.1..sunk.1) | dynamic-update-slice | bytes 2097156 | tf_op jit(solution)/shard_map/while/body/jit(dynamic_update_index_in_dim)/dynamic_update_slice | solution.py:221
  676.5 20.0 %dynamic_update_slice.85 = f32[4,1024,4,64]{1,0,3,2:T(4,128)} dynamic-update-slice(f32[4,1024,4,64]{1,0,3,2:T(4,128)} %get-tuple-element.828, f32[1,1024,4,64]{1,0,3,2:T(1,128)S(1)} %copy-done, s32[]{:T(128)S(6)} %copy.143, s32[]{:T(128)} %constant.263.clone.1..sunk.1, s32[]{:T(128)} %constant.263.clone.1..sunk.1, s32[]{:T(128)} %constant.263.clone.1..sunk.1) | dynamic-update-slice | bytes 2097156 | tf_op jit(solution)/shard_map/while/body/jit(dynamic_update_index_in_dim)/dynamic_update_slice | solution.py:221
  701.7 33.4 %while.47 = (s32[]{:T(128)}, f32[1024,4,64]{0,2,1:T(8,128)S(1)}, f32[1024,4,64]{0,2,1:T(8,128)}, f32[2,512,4,64]{1,3,2,0:T(8,128)}, s32[2]{0:T(128)S(1)}, /*inde...) while((s32[]{:T(128)}, f32[1024,4,64]{0,2,1:T(8,128)S(1)}, ...), condition=%wide.region_10.10_spmd.clone, body=%wide.region_8.9_spmd.clone.sunk | while | flops 1375598592 | bytes 89196952 | solution.py:216
  742.4 19.9 %dynamic_update_slice.84 = f32[4,1024,4,64]{1,0,3,2:T(4,128)} dynamic-update-slice(f32[4,1024,4,64]{1,0,3,2:T(4,128)} %get-tuple-element.827, f32[1,1024,4,64]{1,0,3,2:T(1,128)S(1)} %copy.102, s32[]{:T(128)S(6)} %copy.143, s32[]{:T(128)} %constant.263.clone.1..sunk.1, s32[]{:T(128)} %constant.263.clone.1..sunk.1, s32[]{:T(128)} %constant.263.clone.1..sunk.1) | dynamic-update-slice | bytes 2097156 | tf_op jit(solution)/shard_map/while/body/jit(dynamic_update_index_in_dim)/dynamic_update_slice | solution.py:221
  762.3 20.0 %dynamic_update_slice.85 = f32[4,1024,4,64]{1,0,3,2:T(4,128)} dynamic-update-slice(f32[4,1024,4,64]{1,0,3,2:T(4,128)} %get-tuple-element.828, f32[1,1024,4,64]{1,0,3,2:T(1,128)S(1)} %copy-done, s32[]{:T(128)S(6)} %copy.143, s32[]{:T(128)} %constant.263.clone.1..sunk.1, s32[]{:T(128)} %constant.263.clone.1..sunk.1, s32[]{:T(128)} %constant.263.clone.1..sunk.1) | dynamic-update-slice | bytes 2097156 | tf_op jit(solution)/shard_map/while/body/jit(dynamic_update_index_in_dim)/dynamic_update_slice | solution.py:221
  800.6 13.2 fusion.82
  813.7 13.6 fusion.83
  827.3 13.2 fusion.84
  840.5 36.3 %convert_reduce_fusion = (f32[1024]{0:T(1024)}, bf16[4096,1024]{1,0:T(8,128)(2,1)}) fusion(f32[4096,1024]{1,0:T(8,128)} %fusion.81, f32[1024]{0:T(1024)S(1)} %copy-done.46, bf16[4096,2048]{1,0:T(8,128)(2,1)} %all-gather.21.cloned.1.call-done, bf16[1024,2048]{1,0:T(8,128)(2,1)} %all-gather.19.cloned.1.call-done), kind=kOutput, calls=%fused_computation.68 | convolution fusion | flops 17276338176 | bytes 46145536 | tf_op jit(solution)/shard_map/rd,fd->rf/dot_general | solution.py:169
  876.8 48.7 %add_add_fusion = f32[4096,2048]{1,0:T(8,128)} fusion(f32[4096,2048]{1,0:T(8,128)} %fusion.84, f32[4096,2048]{1,0:T(8,128)} %fusion.82, f32[4096,2048]{1,0:T(8,128)} %fusion.83, bf16[4096,1024]{1,0:T(8,128)(2,1)} %get-tuple-element.433, bf16[2048,1024]{1,0:T(8,128)(2,1)} %all-gather.17.cloned.1.call-done), kind=kOutput, calls=%fused_computation.57 | convolution fusion | flops 17205035008 | bytes 146800640 | tf_op jit(solution)/shard_map/rf,df->rd/dot_general | solution.py:241
  930.4 13.2 fusion.80
  943.6 34.0 %convolution_add_fusion = f32[4096,2048]{1,0:T(8,128)} fusion(f32[4096,2048]{1,0:T(8,128)} %fusion.80, bf16[1024,2048]{1,0:T(8,128)(2,1)S(1)} %copy-done.48, f32[4096,1024]{1,0:T(8,128)} %fusion.81, f32[1024]{0:T(1024)S(1)} %copy-done.46), kind=kOutput, calls=%fused_computation.60 | convolution fusion | flops 17230200832 | bytes 88084480 | tf_op jit(solution)/shard_map/dot_general | solution.py:146
  979.2 9.8 fusion.87
  989.2 12.4 fusion.88
  1001.7 13.0 fusion.86
  1014.8 9.8 fusion.85
  1025.0 24.2 %fusion.89 = f32[2048,1024]{1,0:T(8,128)} fusion(bf16[4096,2048]{1,0:T(8,128)(2,1)} %all-gather.23.cloned.1.call-done, bf16[4096,1024]{1,0:T(8,128)(2,1)} %get-tuple-element.433), kind=kOutput, calls=%fused_computation.152 | convolution fusion | flops 17179869184 | bytes 33554432 | tf_op jit(solution)/shard_map/rd,rf->df/dot_general | solution.py:236
  1049.2 28.8 %fusion.76 = f32[1024,2048]{1,0:T(8,128)} fusion(bf16[4096,2048]{1,0:T(8,128)(2,1)} %all-gather.21.cloned.1.call-done, f32[4096,1024]{1,0:T(8,128)} %fusion.81, f32[1024]{0:T(1024)S(1)} %copy-done.46), kind=kOutput, calls=%fused_computation.141 | convolution fusion | flops 17221812224 | bytes 41947136 | tf_op jit(solution)/shard_map/rf,rd->fd/dot_general | solution.py:165
  1081.0 15.2 all-reduce.1
  1096.2 183.7 %reduce-scatter.11.cloned.1.call-done = f32[512,2048]{1,0:T(8,128)} async-done(((f32[4096,2048]{1,0:T(8,128)}), f32[512,2048]{1,0:T(8,128)}) %reduce-scatter.11.cloned.1.call-update) | async-done | bytes 4194320 | tf_op jit(solution)/shard_map/reduce_scatter | solution.py:237
  1285.3 320.8 %reduce-scatter.9.cloned.1.call-done = f32[512,2048]{1,0:T(8,128)} async-done(((f32[4096,2048]{1,0:T(8,128)}), f32[512,2048]{1,0:T(8,128)}) %reduce-scatter.9.cloned.1.call-update) | async-done | bytes 4194320 | tf_op jit(solution)/shard_map/reduce_scatter | solution.py:144
  1606.2 7.6 convert_reduce_fusion.2
  1613.7 38.3 %all-reduce = (f32[2048]{0:T(1024)}, f32[2048]{0:T(1024)}, f32[2048]{0:T(1024)S(1)}) all-reduce(f32[2048]{0:T(1024)S(1)} %get-tuple-element.359, f32[2048]{0:T(1024)S(1)} %get-tuple-element.361, f32[2048]{0:T(1024)S(1)} %get-tuple-element.460), channel_id=1, replica_groups=mesh['dp'=4,'tensor'=8] {'dp','tensor'}, use_global_device_ids=true, to_apply=%region_16.17 | all-reduce | flops 6144 | bytes 49152 | tf_op jit(solution)/shard_map/psum | solution.py:250
  1652.1 30.9 %reduce-scatter.19.cloned.1.call-done = f32[256,512]{1,0:T(8,128)} async-done(((f32[256,2048]{1,0:T(8,128)}), f32[256,512]{1,0:T(8,128)}) %reduce-scatter.19.cloned.1.call-update) | async-done | bytes 524304 | tf_op jit(solution)/shard_map/reduce_scatter | solution.py:274
  1682.9 38.8 %reduce-scatter.15.cloned.1.call-done = f32[512,256]{1,0:T(8,128)} async-done(((f32[2048,256]{1,0:T(8,128)}), f32[512,256]{1,0:T(8,128)}) %reduce-scatter.15.cloned.1.call-update) | async-done | bytes 524304 | tf_op jit(solution)/shard_map/reduce_scatter | solution.py:271
  1721.7 38.9 %reduce-scatter.13.cloned.1.call-done = f32[512,256]{1,0:T(8,128)} async-done(((f32[2048,256]{1,0:T(8,128)}), f32[512,256]{1,0:T(8,128)}) %reduce-scatter.13.cloned.1.call-update) | async-done | bytes 524304 | tf_op jit(solution)/shard_map/reduce_scatter | solution.py:270
  1760.6 89.9 %reduce-scatter.21.cloned.1.call-done = f32[512,1024]{1,0:T(8,128)} async-done(((f32[2048,1024]{1,0:T(8,128)}), f32[512,1024]{1,0:T(8,128)}) %reduce-scatter.21.cloned.1.call-update) | async-done | bytes 2097168 | tf_op jit(solution)/shard_map/reduce_scatter | solution.py:273
  1850.5 90.2 %reduce-scatter.23.cloned.1.call-done = f32[1024,512]{1,0:T(8,128)} async-done(((f32[1024,2048]{1,0:T(8,128)}), f32[1024,512]{1,0:T(8,128)}) %reduce-scatter.23.cloned.1.call-update) | async-done | bytes 2097168 | tf_op jit(solution)/shard_map/reduce_scatter | solution.py:275
  (478 shorter events, 374.7 us)
Async XLA Ops:
  7.2 185.1 %all-gather.13.cloned.1.call-start = ((), (), s32[]{:S(2)}) async-start(), calls=%async_computation.10 | async-start | bytes 1310720 | tf_op jit(solution)/shard_map/all_gather | solution.py:99
  7.9 214.8 %all-gather.11.cloned.1.call-start = ((), (), s32[]{:S(2)}) async-start(), calls=%async_computation.9 | async-start | bytes 1310720 | tf_op jit(solution)/shard_map/all_gather | solution.py:98
  8.7 244.5 %all-gather.9.cloned.1.call-start = ((), (), s32[]{:S(2)}) async-start(), calls=%async_computation.8 | async-start | bytes 1310720 | tf_op jit(solution)/shard_map/all_gather | solution.py:100
  9.4 383.7 %all-gather.17.cloned.1.call-start = ((), (), s32[]{:S(2)}) async-start(), calls=%async_computation.12 | async-start | bytes 5242880 | tf_op jit(solution)/shard_map/all_gather | solution.py:101
  10.0 407.5 %all-gather.15.cloned.1.call-start = ((), (), s32[]{:S(2)}) async-start(), calls=%async_computation.11 | async-start | bytes 1310720 | tf_op jit(solution)/shard_map/all_gather | solution.py:102
  10.6 406.9 %all-gather.21.cloned.1.call-start = ((), (), s32[]{:S(2)}) async-start(), calls=%async_computation.15 | async-start | bytes 18874368 | tf_op jit(solution)/shard_map/all_gather | solution.py:163
  11.2 829.4 %all-gather.19.cloned.1.call-start = ((), (), s32[]{:S(2)}) async-start(), calls=%async_computation.13 | async-start | bytes 5242880 | tf_op jit(solution)/shard_map/all_gather | solution.py:103
  11.9 965.8 %all-gather.23.cloned.1.call-start = ((), (), s32[]{:S(2)}) async-start(), calls=%async_computation.17 | async-start | bytes 18874368 | tf_op jit(solution)/shard_map/all_gather | solution.py:162
  15.7 107.5 %copy-start.49 = (bf16[256]{0:T(256)(128)(2,1)S(1)}, bf16[256]{0:T(256)(128)(2,1)}, u32[]{:S(2)}) copy-start(bf16[256]{0:T(256)(128)(2,1)} %param.28) | copy-start | bytes 1540
  15.7 107.5 %copy-start.50 = (bf16[256]{0:T(256)(128)(2,1)S(1)}, bf16[256]{0:T(256)(128)(2,1)}, u32[]{:S(2)}) copy-start(bf16[256]{0:T(256)(128)(2,1)} %param.30) | copy-start | bytes 1540
  15.7 107.5 %copy-start.51 = (bf16[256]{0:T(256)(128)(2,1)S(1)}, bf16[256]{0:T(256)(128)(2,1)}, u32[]{:S(2)}) copy-start(bf16[256]{0:T(256)(128)(2,1)} %param.32) | copy-start | bytes 1540
  15.8 107.5 %copy-start.47 = (bf16[1024]{0:T(1024)(128)(2,1)S(1)}, bf16[1024]{0:T(1024)(128)(2,1)}, u32[]{:S(2)}) copy-start(bf16[1024]{0:T(1024)(128)(2,1)} %param.36) | copy-start | bytes 6148
  23.8 48.2 %collective-permute-start = (bf16[512,2048]{1,0:T(8,128)(2,1)}, bf16[512,2048]{1,0:T(8,128)(2,1)S(1)}, u32[]{:S(2)}, u32[]{:S(2)}) collective-permute-start(bf16[512,2048]{1,0:T(8,128)(2,1)} %get-tuple-element.439), channel_id=1, source_target_pairs={{0,1},{1,2},{2,3},{3,4},{4,5},{5,6},{6,7},{7,0},{8,9},{9,10},{10,1... | collective-permute-start | bytes 6291464 | tf_op jit(solution)/shard_map/ppermute | solution.py:19
  24.2 48.4 %collective-permute-start.1 = (bf16[512,2048]{1,0:T(8,128)(2,1)}, bf16[512,2048]{1,0:T(8,128)(2,1)S(1)}, u32[]{:S(2)}, u32[]{:S(2)}) collective-permute-start(bf16[512,2048]{1,0:T(8,128)(2,1)} %get-tuple-element.439), channel_id=1, source_target_pairs={{0,7},{1,0},{2,1},{3,2},{4,3},{5,4},{6,5},{7,6},{8,15},{9,8},{10,9... | collective-permute-start | bytes 6291464 | tf_op jit(solution)/shard_map/ppermute | solution.py:22
  72.0 46.3 %collective-permute-start.2 = (bf16[512,2048]{1,0:T(8,128)(2,1)S(1)}, bf16[512,2048]{1,0:T(8,128)(2,1)}, u32[]{:S(2)}, u32[]{:S(2)}) collective-permute-start(bf16[512,2048]{1,0:T(8,128)(2,1)S(1)} %collective-permute-done), channel_id=1, source_target_pairs={{0,1},{1,2},{2,3},{3,4},{4,5},{5,6},{6,7},{7,0},{8,9},{9,10},{10,1... | collective-permute-start | bytes 6291464 | tf_op jit(solution)/shard_map/ppermute | solution.py:19
  72.6 45.7 %copy-start.17 = (bf16[512,2048]{1,0:T(8,128)(2,1)}, bf16[512,2048]{1,0:T(8,128)(2,1)S(1)}, u32[]{:S(2)}) copy-start(bf16[512,2048]{1,0:T(8,128)(2,1)S(1)} %collective-permute-done.1) | copy-start | bytes 6291460
  72.6 46.5 %collective-permute-start.3 = (bf16[512,2048]{1,0:T(8,128)(2,1)S(1)}, bf16[512,2048]{1,0:T(8,128)(2,1)}, u32[]{:S(2)}, u32[]{:S(2)}) collective-permute-start(bf16[512,2048]{1,0:T(8,128)(2,1)S(1)} %collective-permute-done.1), channel_id=1, source_target_pairs={{0,7},{1,0},{2,1},{3,2},{4,3},{5,4},{6,5},{7,6},{8,15},{9,8},{10,9... | collective-permute-start | bytes 6291464 | tf_op jit(solution)/shard_map/ppermute | solution.py:22
  118.3 44.8 %collective-permute-start.4 = (bf16[512,2048]{1,0:T(8,128)(2,1)}, bf16[512,2048]{1,0:T(8,128)(2,1)}, u32[]{:S(2)}, u32[]{:S(2)}) collective-permute-start(bf16[512,2048]{1,0:T(8,128)(2,1)} %collective-permute-done.2), channel_id=1, source_target_pairs={{0,1},{1,2},{2,3},{3,4},{4,5},{5,6},{6,7},{7,0},{8,9},{9,10},{10,1... | collective-permute-start | bytes 6291464 | tf_op jit(solution)/shard_map/ppermute | solution.py:19
  119.1 57.5 %collective-permute-start.5 = (bf16[512,2048]{1,0:T(8,128)(2,1)}, bf16[512,2048]{1,0:T(8,128)(2,1)}, u32[]{:S(2)}, u32[]{:S(2)}) collective-permute-start(bf16[512,2048]{1,0:T(8,128)(2,1)} %collective-permute-done.3), channel_id=1, source_target_pairs={{0,7},{1,0},{2,1},{3,2},{4,3},{5,4},{6,5},{7,6},{8,15},{9,8},{10,9... | collective-permute-start | bytes 6291464 | tf_op jit(solution)/shard_map/ppermute | solution.py:22
  123.0 1156.9 %reduce-scatter.11.cloned.1.call-start = ((), (), s32[]{:S(2)}) async-start(), calls=%async_computation.16 | async-start | bytes 37748736 | tf_op jit(solution)/shard_map/reduce_scatter | solution.py:237
  123.9 41.6 %copy-start.18 = (bf16[512,2048]{1,0:T(8,128)(2,1)S(1)}, bf16[512,2048]{1,0:T(8,128)(2,1)}, u32[]{:S(2)}) copy-start(bf16[512,2048]{1,0:T(8,128)(2,1)} %copy-done.17) | copy-start | bytes 6291460
  163.1 27.7 %collective-permute-start.6 = (bf16[512,2048]{1,0:T(8,128)(2,1)}, bf16[512,2048]{1,0:T(8,128)(2,1)S(1)}, u32[]{:S(2)}, u32[]{:S(2)}) collective-permute-start(bf16[512,2048]{1,0:T(8,128)(2,1)} %collective-permute-done.4), channel_id=1, source_target_pairs={{0,1},{1,2},{2,3},{3,4},{4,5},{5,6},{6,7},{7,0},{8,9},{9,10},{10,1... | collective-permute-start | bytes 6291464 | tf_op jit(solution)/shard_map/ppermute | solution.py:19
  164.1 115.3 %copy-start.22 = (f32[1024,32]{0,1:T(8,128)}, f32[1024,32]{0,1:T(8,128)S(1)}, u32[]{:S(2)}) copy-start(f32[1024,32]{0,1:T(8,128)S(1)} %get-tuple-element.469) | copy-start | bytes 393220
  393.1 24.4 %copy-start.20 = (bf16[8,512,4,64]{1,3,2,0:T(8,128)(2,1)}, bf16[8,512,4,64]{1,3,2,0:T(8,128)(2,1)S(1)}, u32[]{:S(2)}) copy-start(bf16[8,512,4,64]{1,3,2,0:T(8,128)(2,1)S(1)} %get-tuple-element.277) | copy-start | bytes 6291460
  482.6 22.2 %copy-start = (f32[1,1024,4,64]{1,0,3,2:T(1,128)S(1)}, f32[1,1024,4,64]{1,0,3,2:T(1,128)}, u32[]{:S(2)}) copy-start(f32[1,1024,4,64]{1,0,3,2:T(1,128)} %copy.103) | copy-start | bytes 3145732 | tf_op jit(solution)/shard_map/while
  568.6 22.1 %copy-start = (f32[1,1024,4,64]{1,0,3,2:T(1,128)S(1)}, f32[1,1024,4,64]{1,0,3,2:T(1,128)}, u32[]{:S(2)}) copy-start(f32[1,1024,4,64]{1,0,3,2:T(1,128)} %copy.103) | copy-start | bytes 3145732 | tf_op jit(solution)/shard_map/while
  654.4 22.1 %copy-start = (f32[1,1024,4,64]{1,0,3,2:T(1,128)S(1)}, f32[1,1024,4,64]{1,0,3,2:T(1,128)}, u32[]{:S(2)}) copy-start(f32[1,1024,4,64]{1,0,3,2:T(1,128)} %copy.103) | copy-start | bytes 3145732 | tf_op jit(solution)/shard_map/while
  740.2 22.1 %copy-start = (f32[1,1024,4,64]{1,0,3,2:T(1,128)S(1)}, f32[1,1024,4,64]{1,0,3,2:T(1,128)}, u32[]{:S(2)}) copy-start(f32[1,1024,4,64]{1,0,3,2:T(1,128)} %copy.103) | copy-start | bytes 3145732 | tf_op jit(solution)/shard_map/while
  786.7 40.6 %copy-start.9 = (bf16[32,8,4,1024]{3,1,2,0:T(8,128)(2,1)}, bf16[32,8,4,1024]{3,1,2,0:T(8,128)(2,1)S(1)}, u32[]{:S(2)}) copy-start(bf16[32,8,4,1024]{3,1,2,0:T(8,128)(2,1)S(1)} %copy.97) | copy-start | bytes 6291460
  796.6 17.1 copy-start.13
  800.5 13.2 copy-start.11
  800.5 13.2 copy-start.24
  813.7 13.6 copy-start.27
  827.3 13.2 copy-start.46
  925.5 680.7 %reduce-scatter.9.cloned.1.call-start = ((), (), s32[]{:S(2)}) async-start(), calls=%async_computation.14 | async-start | bytes 37748736 | tf_op jit(solution)/shard_map/reduce_scatter | solution.py:144
  930.4 13.2 copy-start.48
  977.6 674.5 %reduce-scatter.17.cloned.1.call-start = ((), (), s32[]{:S(2)}) async-start(), calls=%async_computation.20 | async-start | bytes 2621440 | tf_op jit(solution)/shard_map/reduce_scatter | solution.py:272
  988.9 694.0 %reduce-scatter.19.cloned.1.call-start = ((), (), s32[]{:S(2)}) async-start(), calls=%async_computation.21 | async-start | bytes 2621440 | tf_op jit(solution)/shard_map/reduce_scatter | solution.py:274
  1001.7 720.0 %reduce-scatter.15.cloned.1.call-start = ((), (), s32[]{:S(2)}) async-start(), calls=%async_computation.19 | async-start | bytes 2621440 | tf_op jit(solution)/shard_map/reduce_scatter | solution.py:271
  1014.7 745.9 %reduce-scatter.13.cloned.1.call-start = ((), (), s32[]{:S(2)}) async-start(), calls=%async_computation.18 | async-start | bytes 2621440 | tf_op jit(solution)/shard_map/reduce_scatter | solution.py:270
  1024.7 825.8 %reduce-scatter.21.cloned.1.call-start = ((), (), s32[]{:S(2)}) async-start(), calls=%async_computation.22 | async-start | bytes 10485760 | tf_op jit(solution)/shard_map/reduce_scatter | solution.py:273
  1049.2 891.5 %reduce-scatter.23.cloned.1.call-start = ((), (), s32[]{:S(2)}) async-start(), calls=%async_computation.23 | async-start | bytes 10485760 | tf_op jit(solution)/shard_map/reduce_scatter | solution.py:275
  1078.1 201.8 %copy-start.2 = (bf16[512,2048]{1,0:T(8,128)(2,1)S(1)}, bf16[512,2048]{1,0:T(8,128)(2,1)}, u32[]{:S(2)}) copy-start(bf16[512,2048]{1,0:T(8,128)(2,1)} %param.23) | copy-start | bytes 6291460
  1078.1 201.8 %copy-start.30 = (f32[2048]{0:T(1024)S(1)}, f32[2048]{0:T(1024)}, u32[]{:S(2)}) copy-start(f32[2048]{0:T(1024)} %copy-done.29) | copy-start | bytes 24580
  1078.1 201.8 %copy-start.33 = (f32[512]{0:T(512)S(1)}, f32[512]{0:T(512)}, u32[]{:S(2)}) copy-start(f32[512]{0:T(512)} %copy-done.32) | copy-start | bytes 6148
  1078.7 204.5 %copy-start.37 = (f32[512]{0:T(512)S(1)}, f32[512]{0:T(512)}, u32[]{:S(2)}) copy-start(f32[512]{0:T(512)} %copy-done.36) | copy-start | bytes 6148
  1078.7 204.5 %copy-start.35 = (f32[512]{0:T(512)S(1)}, f32[512]{0:T(512)}, u32[]{:S(2)}) copy-start(f32[512]{0:T(512)} %copy-done.34) | copy-start | bytes 6148
  1652.0 289.3 %copy-start.40 = (f32[2048]{0:T(1024)}, f32[2048]{0:T(1024)S(1)}, u32[]{:S(2)}) copy-start(f32[2048]{0:T(1024)S(1)} %get-tuple-element.895) | copy-start | bytes 24580
  (58 other events, 139.9 us)
Sparse Core Ops, SparseCore 0:
  9.9 29.3 all-gather.12
  41.1 26.6 all-gather.10
  69.6 26.6 all-gather.8
  97.9 52.6 all-gather.16
  152.3 26.4 all-gather.14
  180.3 151.1 all-gather.20
  333.3 54.6 all-gather.18
  390.2 151.1 all-gather.22
  925.6 354.2 reduce-scatter.10
  1282.2 323.8 reduce-scatter.8
  1609.7 34.3 reduce-scatter.16
  1647.7 35.1 reduce-scatter.18
  1686.5 35.1 reduce-scatter.14
  1725.4 35.1 reduce-scatter.12
  1764.1 86.3 reduce-scatter.20
  1854.3 86.3 reduce-scatter.22
